TPU v7x, 32 devices: a whole 2x2x4 slice. The times are simulated.
32 devices in a mesh: rep: 4 (over y, x), fsdp: 8 (over z, core).
Axes of the slice: x: 2, y: 2, z: 4, core: 2. Of those that a mesh axis runs over, the one named last changes fastest.
Arguments:
- tokens: bfloat16 [32, 256, 1152], P(('rep', 'fsdp')), may hold values from -6 to 6
- conditioning: bfloat16 [32, 4, 1152], P(('rep', 'fsdp')), may hold values from -6 to 6
- segment_ids: int32 [32, 256], P(('rep', 'fsdp')), may hold values from 0 to 3, as said below
- heights: int32 [32, 4], P(('rep', 'fsdp')), may hold values from 4 to 32, as said below
- widths: int32 [32, 4], P(('rep', 'fsdp')), may hold values from 4 to 32, as said below
- pad_mask: int32 [32, 256], P(('rep', 'fsdp')), may hold values from 0 to 1, as said below
- modulation_weight: bfloat16 [1152, 6912], P(None, 'fsdp'), may hold values from -0.1875 to 0.1875
- modulation_bias: bfloat16 [6912], P('fsdp'), may hold values from -3 to 3
- projection_weight: bfloat16 [1152, 3456], P('fsdp'), may hold values from -0.1875 to 0.1875
- projection_bias: bfloat16 [3456], P('fsdp'), may hold values from -3 to 3
- output_weight: bfloat16 [1152, 1152], P('fsdp'), may hold values from -1.5 to 1.5
- output_bias: bfloat16 [1152], P('fsdp'), may hold values from -3 to 3
- gate_weight: bfloat16 [1152, 3072], P('fsdp'), may hold values from -0.1875 to 0.1875
- up_weight: bfloat16 [1152, 3072], P('fsdp'), may hold values from -0.1875 to 0.1875
- down_weight: bfloat16 [3072, 1152], P('fsdp'), may hold values from -0.109375 to 0.109375
- cotangent: bfloat16 [32, 256, 1152], P(('rep', 'fsdp')), may hold values from -6 to 6
Outputs:
- block_output: bfloat16 [32, 256, 1152], P(('rep', 'fsdp'))
- tokens_gradient: float32 [32, 256, 1152], P(('rep', 'fsdp'))
- conditioning_gradient: float32 [32, 4, 1152], P(('rep', 'fsdp'))
- modulation_weight_gradient: float32 [1152, 6912], P(None, 'fsdp')
- modulation_bias_gradient: float32 [6912], P('fsdp')
- projection_weight_gradient: float32 [1152, 3456], P('fsdp')
- projection_bias_gradient: float32 [3456], P('fsdp')
- output_weight_gradient: float32 [1152, 1152], P('fsdp')
- output_bias_gradient: float32 [1152], P('fsdp')
- gate_weight_gradient: float32 [1152, 3072], P('fsdp')
- up_weight_gradient: float32 [1152, 3072], P('fsdp')
- down_weight_gradient: float32 [3072, 1152], P('fsdp')
Inputs may be any that keep to these rules, and one draw needn't show every extreme that they name: `segment_ids`: in each row the used image slots 0, 1, ... lie end to end in slot order, slot k covering heights[k] * widths[k] tokens; tokens after the last image carry the id of the first unused slot. `heights`: each slot's grid holds 64 to 256 tokens with aspect between 1:4 and 4:1; a row uses as many leading slots as fit its 256 tokens, at least one; unused slots hold such grids too. `widths`: as for heights. `pad_mask`: 1 exactly on the tokens of the row's used images, 0 on the tokens after them.
All inputs are finite; a program needn't handle non-finite values.
Results may differ from a plain program's by a relative error of at most 0.023.
The roundings to bfloat16 on the way count: a program that leaves them out, or rounds other values in their place, can miss the bound.
Values may be sent and summed in bfloat16 or wider, within the bound.
No kernel may reach another device: no remote copies, remote signals or barrier semaphores. Data moves between devices by JAX's collectives and lax.ppermute only.
A program may use at most 384 MiB of HBM per device.

v0:
```python
import math

import jax
import jax.numpy as jnp
from jax import lax
from jax.sharding import PartitionSpec as P

HEADS = 16


def token_places(segment_ids, heights, widths):
    slot_count = heights.shape[1]
    token_count = segment_ids.shape[1]
    slot_ids = jnp.arange(slot_count, dtype=jnp.int32)
    member_ints = (segment_ids[:, :, None] == slot_ids[None, None, :]).astype(jnp.int32)
    before_ints = (slot_ids[None, None, :] < segment_ids[:, :, None]).astype(jnp.int32)
    grid_sizes = heights * widths
    starts = jnp.sum(before_ints * grid_sizes[:, None, :], axis=2)
    offsets = jnp.arange(token_count, dtype=jnp.int32)[None, :] - starts
    row_width = jnp.sum(member_ints * widths[:, None, :], axis=2)
    return (member_ints.astype(jnp.float32), offsets // row_width, offsets % row_width)


def rotary_tables(grid_rows, grid_columns, head_width):
    pair_count = head_width // 4
    frequency = 10000.0 ** (-jnp.arange(pair_count, dtype=jnp.float32) / pair_count)
    places = jnp.stack([grid_rows, grid_columns], axis=-1).astype(jnp.float32)
    turned = places[..., None] * frequency
    return (jnp.cos(turned)[:, :, None], jnp.sin(turned)[:, :, None])


def rotate(vectors, cosine_table, sine_table):
    full_shape = vectors.shape
    split_view = vectors.reshape(full_shape[:-1] + (2, 2, full_shape[-1] // 4))
    first_half = split_view[..., 0, :]
    second = split_view[..., 1, :]
    turned = jnp.stack(
        [
            first_half * cosine_table - second * sine_table,
            first_half * sine_table + second * cosine_table,
        ],
        axis=-2,
    )
    return turned.reshape(full_shape)


def normalize_keep(values):
    centered = values - jnp.mean(values, axis=-1, keepdims=True)
    variance = jnp.mean(centered * centered, axis=-1, keepdims=True)
    inverse = lax.rsqrt(variance + 1e-06)
    return (centered * inverse, inverse)


def normalize_back(normed, inverse, upstream):
    return inverse * (
        upstream
        - jnp.mean(upstream, axis=-1, keepdims=True)
        - normed * jnp.mean(upstream * normed, axis=-1, keepdims=True)
    )


def matmul(left, right):
    return jnp.dot(left, right, preferred_element_type=jnp.float32)


def matmul_right_t(left, right):
    return lax.dot_general(
        left, right, (((left.ndim - 1,), (1,)), ((), ())), preferred_element_type=jnp.float32
    )


def matmul_left_t(left, right):
    return lax.dot_general(
        left, right, (((0,), (0,)), ((), ())), preferred_element_type=jnp.float32
    )


def silu_slope(values):
    sigmoid = jax.nn.sigmoid(values)
    return sigmoid * (1.0 + values * (1.0 - sigmoid))


def on_device(
    tokens,
    conditioning,
    segment_ids,
    heights,
    widths,
    pad_mask,
    modulation_weight,
    modulation_bias,
    projection_weight,
    projection_bias,
    output_weight,
    output_bias,
    gate_weight,
    up_weight,
    down_weight,
    cotangent,
):
    row_count, token_count, model_width = tokens.shape
    slot_count = conditioning.shape[1]
    head_width = model_width // HEADS
    token_total = row_count * token_count
    score_scale = 1.0 / math.sqrt(head_width)
    members, grid_rows, grid_columns = token_places(segment_ids, heights, widths)
    cosine_table, sine_table = rotary_tables(grid_rows, grid_columns, head_width)
    cond_float = conditioning.astype(jnp.float32)
    table_full, table_bias = (
        lax.all_gather(modulation_weight, "fsdp", axis=1, tiled=True),
        lax.all_gather(modulation_bias, "fsdp", axis=0, tiled=True),
    )
    activated = jax.nn.silu(cond_float).astype(jnp.bfloat16)
    modulation = lax.dot_general(
        activated, table_full, (((2,), (0,)), ((), ())), preferred_element_type=jnp.float32
    ) + table_bias.astype(jnp.float32)
    per_token = jnp.einsum("rsk,rkc->rsc", members, modulation, precision=lax.Precision.HIGHEST)
    shift_one, scale_one, gate_one, shift_two, scale_two, gate_two = jnp.split(
        per_token, 6, axis=-1
    )
    tokens_float = tokens.astype(jnp.float32)
    normed_one, inverse_one = normalize_keep(tokens_float)
    hidden_one = (
        (normed_one * (1.0 + scale_one) + shift_one)
        .astype(jnp.bfloat16)
        .reshape(token_total, model_width)
    )
    attention_set = (
        lax.all_gather(projection_weight, "fsdp", axis=0, tiled=True),
        lax.all_gather(projection_bias, "fsdp", axis=0, tiled=True),
        lax.all_gather(output_weight, "fsdp", axis=0, tiled=True),
        lax.all_gather(output_bias, "fsdp", axis=0, tiled=True),
    )
    projected = matmul(hidden_one, attention_set[0]) + attention_set[1].astype(jnp.float32)
    query_part, key_part, value_part = jnp.split(
        projected.reshape(row_count, token_count, 3 * model_width), 3, axis=-1
    )
    head_shape = (row_count, token_count, HEADS, head_width)
    query_rot = rotate(query_part.reshape(head_shape), cosine_table, sine_table).astype(
        jnp.bfloat16
    )
    key_rot = rotate(key_part.reshape(head_shape), cosine_table, sine_table).astype(jnp.bfloat16)
    value_low = value_part.reshape(head_shape).astype(jnp.bfloat16)
    same_image = (segment_ids[:, :, None] == segment_ids[:, None, :])[:, None]

    def masked_scores():
        raw_scores = (
            jnp.einsum("rqhe,rkhe->rhqk", query_rot, key_rot, preferred_element_type=jnp.float32)
            * score_scale
        )
        return jnp.where(same_image, raw_scores, -1e30)

    scores = masked_scores()
    score_top = jnp.max(scores, axis=-1, keepdims=True)
    exponent = jnp.exp(scores - score_top)
    exp_total = jnp.sum(exponent, axis=-1, keepdims=True)
    attention_probs = exponent / exp_total
    log_total = score_top + jnp.log(exp_total)
    attended = jnp.einsum(
        "rhqk,rkhe->rqhe",
        attention_probs.astype(jnp.bfloat16),
        value_low,
        preferred_element_type=jnp.float32,
    )
    attended = attended.astype(jnp.bfloat16).reshape(token_total, model_width)
    branch = (matmul(attended, attention_set[2]) + attention_set[3].astype(jnp.float32)).reshape(
        row_count, token_count, model_width
    )
    middle = tokens_float + gate_one * branch
    normed_two, inverse_two = normalize_keep(middle)
    hidden_two = (
        (normed_two * (1.0 + scale_two) + shift_two)
        .astype(jnp.bfloat16)
        .reshape(token_total, model_width)
    )
    feed_set = (
        lax.all_gather(gate_weight, "fsdp", axis=0, tiled=True),
        lax.all_gather(up_weight, "fsdp", axis=0, tiled=True),
        lax.all_gather(down_weight, "fsdp", axis=0, tiled=True),
    )
    gate_value = matmul(hidden_two, feed_set[0])
    up_value = matmul(hidden_two, feed_set[1])
    hidden_three = (jax.nn.silu(gate_value) * up_value).astype(jnp.bfloat16)
    feed = matmul(hidden_three, feed_set[2]).reshape(row_count, token_count, model_width)
    block_output = (middle + gate_two * feed).astype(jnp.bfloat16)
    ff_width = hidden_three.shape[1]
    masked = cotangent.astype(jnp.float32) * pad_mask.astype(jnp.float32)[:, :, None]
    feed_set = (
        lax.all_gather(gate_weight, "fsdp", axis=0, tiled=True),
        lax.all_gather(up_weight, "fsdp", axis=0, tiled=True),
        lax.all_gather(down_weight, "fsdp", axis=0, tiled=True),
    )
    feed_back = (gate_two * masked).astype(jnp.bfloat16).reshape(token_total, model_width)
    gate_two_back = masked * feed
    down_gradient = lax.psum_scatter(
        matmul_left_t(hidden_three, feed_back).astype(jnp.bfloat16),
        "fsdp",
        scatter_dimension=0,
        tiled=True,
    )
    hidden_back = matmul_right_t(feed_back, feed_set[2])
    gate_back = (hidden_back * up_value * silu_slope(gate_value)).astype(jnp.bfloat16)
    up_back = (hidden_back * jax.nn.silu(gate_value)).astype(jnp.bfloat16)
    hidden_two_back = (
        matmul_right_t(gate_back, feed_set[0]) + matmul_right_t(up_back, feed_set[1])
    ).reshape(row_count, token_count, model_width)
    middle_back = masked + normalize_back(
        normed_two, inverse_two, hidden_two_back * (1.0 + scale_two)
    )
    gate_one_back = middle_back * branch
    branch_back = (middle_back * gate_one).astype(jnp.bfloat16).reshape(token_total, model_width)
    attention_set = (
        lax.all_gather(projection_weight, "fsdp", axis=0, tiled=True),
        lax.all_gather(projection_bias, "fsdp", axis=0, tiled=True),
        lax.all_gather(output_weight, "fsdp", axis=0, tiled=True),
        lax.all_gather(output_bias, "fsdp", axis=0, tiled=True),
    )
    output_bias_gradient = jnp.sum(branch_back.astype(jnp.float32), axis=0)
    attended_back = (
        matmul_right_t(branch_back, attention_set[2]).astype(jnp.bfloat16).reshape(head_shape)
    )
    scores = masked_scores()
    attention_probs = jnp.exp(scores - log_total)
    probs_low = attention_probs.astype(jnp.bfloat16)
    probs_back = jnp.einsum(
        "rqhe,rkhe->rhqk", attended_back, value_low, preferred_element_type=jnp.float32
    )
    value_back = jnp.einsum(
        "rhqk,rqhe->rkhe", probs_low, attended_back, preferred_element_type=jnp.float32
    )
    scores_back = attention_probs * (
        probs_back - jnp.sum(attention_probs * probs_back, axis=-1, keepdims=True)
    )
    scores_back = scores_back.astype(jnp.bfloat16)
    query_back = (
        jnp.einsum("rhqk,rkhe->rqhe", scores_back, key_rot, preferred_element_type=jnp.float32)
        * score_scale
    )
    key_back = (
        jnp.einsum("rhqk,rqhe->rkhe", scores_back, query_rot, preferred_element_type=jnp.float32)
        * score_scale
    )
    query_back = rotate(query_back, cosine_table, -sine_table)
    key_back = rotate(key_back, cosine_table, -sine_table)
    projected_back = jnp.concatenate(
        [
            query_back.reshape(token_total, model_width),
            key_back.reshape(token_total, model_width),
            value_back.reshape(token_total, model_width),
        ],
        axis=-1,
    ).astype(jnp.bfloat16)
    projection_bias_gradient = jnp.sum(projected_back.astype(jnp.float32), axis=0)
    row_sums = lax.psum_scatter(
        jnp.concatenate(
            [
                matmul_left_t(hidden_two, gate_back),
                matmul_left_t(hidden_two, up_back),
                matmul_left_t(hidden_one, projected_back),
                matmul_left_t(attended, branch_back),
            ],
            axis=1,
        ).astype(jnp.bfloat16),
        "fsdp",
        scatter_dimension=0,
        tiled=True,
    ).astype(jnp.float32)
    gate_gradient = row_sums[:, :ff_width]
    up_gradient = row_sums[:, ff_width : 2 * ff_width]
    projection_gradient = row_sums[:, 2 * ff_width : 2 * ff_width + 3 * model_width]
    output_gradient = row_sums[:, 2 * ff_width + 3 * model_width :]
    hidden_one_back = matmul_right_t(projected_back, attention_set[0]).reshape(
        row_count, token_count, model_width
    )
    tokens_gradient = middle_back + normalize_back(
        normed_one, inverse_one, hidden_one_back * (1.0 + scale_one)
    )
    per_token_back = jnp.concatenate(
        [
            hidden_one_back,
            hidden_one_back * normed_one,
            gate_one_back,
            hidden_two_back,
            hidden_two_back * normed_two,
            gate_two_back,
        ],
        axis=-1,
    )
    modulation_back = jnp.einsum(
        "rsk,rsc->rkc", members, per_token_back, precision=lax.Precision.HIGHEST
    ).astype(jnp.bfloat16)
    table_bias_term = jnp.sum(modulation_back.astype(jnp.float32), axis=(0, 1))
    flat_slots = row_count * slot_count
    activated_flat = activated.reshape(flat_slots, model_width)
    back_flat = modulation_back.reshape(flat_slots, 6 * model_width)
    table_gradient = (
        lax.psum_scatter(
            matmul_left_t(back_flat, activated_flat).astype(jnp.bfloat16),
            "fsdp",
            scatter_dimension=0,
            tiled=True,
        )
        .astype(jnp.float32)
        .T
    )
    activated_back = lax.dot_general(
        modulation_back, table_full, (((2,), (1,)), ((), ())), preferred_element_type=jnp.float32
    )
    table_bias_gradient, projection_bias_gradient, output_bias_gradient = (
        lax.psum_scatter(
            table_bias_term.astype(jnp.bfloat16), "fsdp", scatter_dimension=0, tiled=True
        ).astype(jnp.float32),
        lax.psum_scatter(
            projection_bias_gradient.astype(jnp.bfloat16), "fsdp", scatter_dimension=0, tiled=True
        ).astype(jnp.float32),
        lax.psum_scatter(
            output_bias_gradient.astype(jnp.bfloat16), "fsdp", scatter_dimension=0, tiled=True
        ).astype(jnp.float32),
    )
    conditioning_gradient = activated_back * silu_slope(cond_float)
    summed = (
        lax.psum(table_gradient.astype(jnp.bfloat16), "rep").astype(jnp.float32),
        lax.psum(table_bias_gradient.astype(jnp.bfloat16), "rep").astype(jnp.float32),
        lax.psum(projection_gradient.astype(jnp.bfloat16), "rep").astype(jnp.float32),
        lax.psum(projection_bias_gradient.astype(jnp.bfloat16), "rep").astype(jnp.float32),
        lax.psum(output_gradient.astype(jnp.bfloat16), "rep").astype(jnp.float32),
        lax.psum(output_bias_gradient.astype(jnp.bfloat16), "rep").astype(jnp.float32),
        lax.psum(gate_gradient.astype(jnp.bfloat16), "rep").astype(jnp.float32),
        lax.psum(up_gradient.astype(jnp.bfloat16), "rep").astype(jnp.float32),
        lax.psum(down_gradient, "rep").astype(jnp.float32),
    )
    return (
        block_output,
        tokens_gradient,
        conditioning_gradient,
        summed[0],
        summed[1],
        summed[2],
        summed[3],
        summed[4],
        summed[5],
        summed[6],
        summed[7],
        summed[8],
    )


def solution(mesh):
    in_specs = (
        P(("rep", "fsdp"), None, None),
        P(("rep", "fsdp"), None, None),
        P(("rep", "fsdp"), None),
        P(("rep", "fsdp"), None),
        P(("rep", "fsdp"), None),
        P(("rep", "fsdp"), None),
        P(None, "fsdp"),
        P("fsdp"),
        P("fsdp", None),
        P("fsdp"),
        P("fsdp", None),
        P("fsdp"),
        P("fsdp", None),
        P("fsdp", None),
        P("fsdp", None),
        P(("rep", "fsdp"), None, None),
    )
    out_specs = (
        P(("rep", "fsdp"), None, None),
        P(("rep", "fsdp"), None, None),
        P(("rep", "fsdp"), None, None),
        P(None, "fsdp"),
        P("fsdp"),
        P("fsdp", None),
        P("fsdp"),
        P("fsdp", None),
        P("fsdp"),
        P("fsdp", None),
        P("fsdp", None),
        P("fsdp", None),
    )
    return jax.shard_map(
        on_device, mesh=mesh, in_specs=in_specs, out_specs=out_specs, check_vma=False
    )
```

profile of v0, /device:TPU:0, one launch (start us, length us, event | category | flops | bytes accessed | tf_op | source)
XLA Modules:
  0.0 1219.1 jit_solution(7360849966451831620)
XLA Ops:
  14.7 31.3 %all-reduce.7 = (bf16[6912]{0:T(1024)(128)(2,1)S(1)}, bf16[3456]{0:T(1024)(128)(2,1)S(1)}, bf16[1152]{0:T(1024)(128)(2,1)S(1)}) all-reduce(bf16[6912]{0:T(1024)(128)(2,1)S(1)} %dynamic-update-slice, bf16[3456]{0:T(1024)(128)(2,1)S(1)} %dynamic-update-slice.1, ...), channel_id=1, replica_groups=mesh['rep'=4,'fsdp'=8] {'fsdp'}, use_global_device_ids=true, to_apply=%add | all-reduce | flops 11520 | bytes 46080
  49.0 107.9 %all-gather.7.cloned.1.call-done = bf16[1152,6912]{0,1:T(8,128)(2,1)} async-done(((bf16[1152,864]{0,1:T(8,128)(2,1)}), bf16[1152,6912]{0,1:T(8,128)(2,1)}) %all-gather.7.cloned.1.call-update) | async-done | bytes 15925264 | tf_op jit(solution)/shard_map/all_gather | solution.py:110
  156.9 9.7 convolution_add_fusion
  166.6 5.8 convolution_bitcast_fusion
  172.4 2.9 copy-done.2
  175.7 59.7 %all-gather.9.cloned.1.call-done = bf16[1152,3456]{1,0:T(8,128)(2,1)} async-done(((bf16[144,3456]{1,0:T(8,128)(2,1)}), bf16[1152,3456]{1,0:T(8,128)(2,1)}) %all-gather.9.cloned.1.call-update) | async-done | bytes 7962640 | tf_op jit(solution)/shard_map/all_gather | solution.py:129
  235.4 5.8 fusion.1
  244.4 3.3 copy.88
  247.7 3.5 subtract_convert_fusion.3
  251.2 3.6 pad_maximum_fusion.2
  260.0 9.8 all-gather.11.cloned.1.call-done
  269.8 4.2 fusion.62
  274.9 2.5 fusion.35
  277.4 64.2 %all-gather.13.cloned.1.call-done = bf16[1152,3072]{1,0:T(8,128)(2,1)} async-done(((bf16[144,3072]{1,0:T(8,128)(2,1)}), bf16[1152,3072]{1,0:T(8,128)(2,1)}) %all-gather.13.cloned.1.call-update) | async-done | bytes 7077904 | tf_op jit(solution)/shard_map/all_gather | solution.py:177
  341.6 6.9 fusion.70
  348.5 64.5 %all-gather.15.cloned.1.call-done = bf16[1152,3072]{1,0:T(8,128)(2,1)} async-done(((bf16[144,3072]{1,0:T(8,128)(2,1)}), bf16[1152,3072]{1,0:T(8,128)(2,1)}) %all-gather.15.cloned.1.call-update) | async-done | bytes 7077904 | tf_op jit(solution)/shard_map/all_gather | solution.py:178
  413.0 6.9 fusion.71
  419.9 64.5 %all-gather.17.cloned.1.call-done = bf16[3072,1152]{1,0:T(8,128)(2,1)} async-done(((bf16[384,1152]{1,0:T(8,128)(2,1)}), bf16[3072,1152]{1,0:T(8,128)(2,1)}) %all-gather.17.cloned.1.call-update) | async-done | bytes 7077904 | tf_op jit(solution)/shard_map/all_gather | solution.py:179
  484.3 9.2 multiply_convert_fusion.1
  493.6 6.9 fusion.72
  500.6 5.4 convolution_bitcast_fusion.2
  506.1 3.3 fusion.59
  509.4 2.2 fusion.61
  516.4 3.8 multiply_reduce_fusion
  525.0 5.3 convolution_convert_fusion.3
  530.4 4.9 convolution_convert_fusion.4
  535.3 2.4 convolution_convert_fusion.6
  539.4 3.3 subtract_convert_fusion.1
  542.7 3.8 maximum_reduce_fusion
  546.5 2.2 reshape_reshape.16
  548.7 5.2 maximum_reduce_fusion.1
  555.9 6.9 convolution_convert_fusion.1
  562.8 17.6 %pad_maximum_fusion = bf16[1152,10752]{1,0:T(8,128)(2,1)} fusion(bf16[1152,1152]{1,0:T(8,128)(2,1)} %convolution_convert_fusion.6, bf16[1152,3456]{1,0:T(8,128)(2,1)} %convolution_convert_fusion.1, bf16[1152,3072]{1,0:T(8,128)(2,1)} %convolution_convert_fusion.3, bf16[1152,3072]{1,0:T(8,128)(2,1)} %convolution_convert_fusion.4), kind=kLoop, calls=%fused_computation.1 | loop fusion | flops 99090432 | bytes 49545216 | tf_op jit(solution)/shard_map/concatenate | solution.py:255
  580.5 7.2 convolution_convert_fusion.2
  588.8 6.7 fusion.60
  595.6 2.9 fusion.30
  601.0 3.4 fusion.69
  604.4 7.9 convolution_convert_fusion
  612.4 210.3 %reduce-scatter.6.cloned.1.call-done = bf16[144,10752]{1,0:T(8,128)(2,1)} async-done(((bf16[1152,10752]{1,0:T(8,128)(2,1)}), bf16[144,10752]{1,0:T(8,128)(2,1)}) %reduce-scatter.6.cloned.1.call-update) | async-done | bytes 3096592 | tf_op jit(solution)/shard_map/reduce_scatter | solution.py:254
  822.7 2.2 slice.60
  826.6 2.7 fusion.64
  829.4 71.3 %reduce-scatter.8.cloned.1.call-done = bf16[384,1152]{1,0:T(8,128)(2,1)} async-done(((bf16[3072,1152]{1,0:T(8,128)(2,1)}), bf16[384,1152]{1,0:T(8,128)(2,1)}) %reduce-scatter.8.cloned.1.call-update) | async-done | bytes 884752 | tf_op jit(solution)/shard_map/reduce_scatter | solution.py:195
  900.7 161.6 %reduce-scatter.4.cloned.1.call-done = bf16[864,1152]{1,0:T(8,128)(2,1)} async-done(((bf16[6912,1152]{1,0:T(8,128)(2,1)}), bf16[864,1152]{1,0:T(8,128)(2,1)}) %reduce-scatter.4.cloned.1.call-update) | async-done | bytes 1990672 | tf_op jit(solution)/shard_map/reduce_scatter | solution.py:297
  1065.1 26.1 %all-reduce.6 = (bf16[6912]{0:T(1024)(128)(2,1)S(1)}, bf16[3456]{0:T(1024)(128)(2,1)S(1)}, bf16[1152]{0:T(1024)(128)(2,1)S(1)}) all-reduce(bf16[6912]{0:T(1024)(128)(2,1)S(1)} %get-tuple-element.81, bf16[3456]{0:T(1024)(128)(2,1)S(1)} %fusion.58, bf16[1152]{0:T(1024)(128)(2,1)S(1)} %copy-done.53), channel_id=3, replica_groups=mesh['rep'=4,'fsdp'=8] {'fsdp'}, use_global_device_ids=true, to_apply=%region_16.17.clone | all-reduce | flops 11520 | bytes 46080
  1091.4 10.3 all-reduce.8
  1103.5 8.5 fusion.7
  1112.0 89.7 %all-reduce.12.cloned.1.call-done = (bf16[1152,864]{0,1:T(8,128)(2,1)}, bf16[144,3456]{1,0:T(8,128)(2,1)}, bf16[144,1152]{1,0:T(8,128)(2,1)}, bf16[144,3072]{1,0...) async-done(((bf16[1152,864]{0,1:T(8,128)(2,1)}, bf16[144,3456]{1,0:T(8,128)(2,1)}, bf16[144,1152]{1,0:T(8,128)(2,1)}, bf16[144,3072]{1,0:T(8,128)(2,1)}, ...) | async-done | bytes 5971984 | tf_op jit(solution)/shard_map/psum | solution.py:322
  1201.7 3.8 convert_element_type.250
  (228 shorter events, 45.6 us)
Async XLA Ops:
  7.2 149.7 %all-gather.7.cloned.1.call-start = ((), (), s32[]{:S(2)}) async-start(), calls=%async_computation.3 | async-start | bytes 17915904 | tf_op jit(solution)/shard_map/all_gather | solution.py:110
  7.9 3.4 copy-start.58
  7.9 227.5 %all-gather.9.cloned.1.call-start = ((), (), s32[]{:S(2)}) async-start(), calls=%async_computation.4 | async-start | bytes 8957952 | tf_op jit(solution)/shard_map/all_gather | solution.py:129
  8.7 5.3 copy-start.59
  8.7 5.5 copy-start.60
  8.7 5.7 copy-start.63
  8.7 37.3 %copy-start.61 = (s32[1,256]{1,0:T(1,128)S(1)}, s32[1,256]{1,0:T(1,128)}, u32[]{:S(2)}) copy-start(s32[1,256]{1,0:T(1,128)} %param.21) | copy-start | bytes 3076
  8.7 37.8 %copy-start.62 = (s32[1,4]{1,0:T(1,128)S(1)}, s32[1,4]{1,0:T(1,128)}, u32[]{:S(2)}) copy-start(s32[1,4]{1,0:T(1,128)} %param.20) | copy-start | bytes 52
  8.7 37.8 %copy-start.64 = (s32[1,4]{1,0:T(1,128)S(1)}, s32[1,4]{1,0:T(1,128)}, u32[]{:S(2)}) copy-start(s32[1,4]{1,0:T(1,128)} %param.19) | copy-start | bytes 52
  8.7 37.8 %copy-start.44 = (s32[1,256]{1,0:T(1,128)S(1)}, s32[1,256]{1,0:T(1,128)}, u32[]{:S(2)}) copy-start(s32[1,256]{1,0:T(1,128)} %param.18) | copy-start | bytes 3076
  8.7 38.2 %copy-start.3 = (bf16[1,256,1152]{2,1,0:T(8,128)(2,1)S(1)}, bf16[1,256,1152]{2,1,0:T(8,128)(2,1)}, u32[]{:S(2)}) copy-start(bf16[1,256,1152]{2,1,0:T(8,128)(2,1)} %param.16) | copy-start | bytes 1769476
  8.8 261.0 %all-gather.11.cloned.1.call-start = ((), (), s32[]{:S(2)}) async-start(), calls=%async_computation.5 | async-start | bytes 2985984 | tf_op jit(solution)/shard_map/all_gather | solution.py:131
  9.5 332.1 %all-gather.13.cloned.1.call-start = ((), (), s32[]{:S(2)}) async-start(), calls=%async_computation.6 | async-start | bytes 7962624 | tf_op jit(solution)/shard_map/all_gather | solution.py:177
  10.1 146.8 %copy-start.39 = (bf16[1,4,1152]{2,1,0:T(4,128)(2,1)S(1)}, bf16[1,4,1152]{2,1,0:T(4,128)(2,1)}, u32[]{:S(2)}) copy-start(bf16[1,4,1152]{2,1,0:T(4,128)(2,1)} %param.17) | copy-start | bytes 27652
  10.1 402.9 %all-gather.15.cloned.1.call-start = ((), (), s32[]{:S(2)}) async-start(), calls=%async_computation.7 | async-start | bytes 7962624 | tf_op jit(solution)/shard_map/all_gather | solution.py:178
  10.7 473.7 %all-gather.17.cloned.1.call-start = ((), (), s32[]{:S(2)}) async-start(), calls=%async_computation.8 | async-start | bytes 7962624 | tf_op jit(solution)/shard_map/all_gather | solution.py:179
  11.2 811.4 %reduce-scatter.6.cloned.1.call-start = ((), (), s32[]{:S(2)}) async-start(), calls=%async_computation.10 | async-start | bytes 27869184 | tf_op jit(solution)/shard_map/reduce_scatter | solution.py:254
  47.1 125.3 %copy-start.54 = (f32[256]{0:T(256)}, f32[256]{0:T(256)S(1)}, u32[]{:S(2)}) copy-start(f32[256]{0:T(256)S(1)} %broadcast_multiply_fusion.5) | copy-start | bytes 3076
  47.4 125.0 %copy-start.56 = (f32[256]{0:T(256)}, f32[256]{0:T(256)S(1)}, u32[]{:S(2)}) copy-start(f32[256]{0:T(256)S(1)} %add_rsqrt_fusion.1) | copy-start | bytes 3076
  175.7 65.5 %copy-start.19 = (bf16[256,1152]{1,0:T(8,128)(2,1)}, bf16[256,1152]{1,0:T(8,128)(2,1)S(1)}, u32[]{:S(2)}) copy-start(bf16[256,1152]{1,0:T(8,128)(2,1)S(1)} %fusion.37) | copy-start | bytes 1769476
  260.0 14.0 %copy-start.17 = (bf16[16,72,256]{2,1,0:T(8,128)(2,1)}, bf16[16,72,256]{2,1,0:T(8,128)(2,1)S(1)}, u32[]{:S(2)}) copy-start(bf16[16,72,256]{2,1,0:T(8,128)(2,1)S(1)} %fusion.20) | copy-start | bytes 1769476
  269.8 5.1 copy-start.7
  269.8 5.1 copy-start.50
  277.4 207.0 %copy-start.22 = (bf16[256,1152]{1,0:T(8,128)(2,1)}, bf16[256,1152]{1,0:T(8,128)(2,1)S(1)}, u32[]{:S(2)}) copy-start(bf16[256,1152]{1,0:T(8,128)(2,1)S(1)} %get-tuple-element.39) | copy-start | bytes 1769476
  493.5 7.0 copy-start.30
  493.6 7.0 copy-start.20
  493.6 12.4 %copy-start.5 = (bf16[256,3072]{1,0:T(8,128)(2,1)}, bf16[256,3072]{1,0:T(8,128)(2,1)S(1)}, u32[]{:S(2)}) copy-start(bf16[256,3072]{1,0:T(8,128)(2,1)S(1)} %get-tuple-element.41) | copy-start | bytes 4718596
  493.6 12.4 %slice-start = ((s8[7077888]{0:T(1024)(128)(4,1)}), s8[4194304]{0:T(1024)(128)(4,1)S(1)}, s32[]{:S(2)}) async-start(s8[7077888]{0:T(1024)(128)(4,1)} %bitcast.117), calls=%async_computation.13 | async-start | bytes 8388608
  493.6 12.4 %slice-start.2 = ((s8[7077888]{0:T(1024)(128)(4,1)}), s8[4194304]{0:T(1024)(128)(4,1)S(1)}, s32[]{:S(2)}) async-start(s8[7077888]{0:T(1024)(128)(4,1)} %bitcast.119), calls=%async_computation.15 | async-start | bytes 8388608
  500.6 5.4 slice-start.1
  500.6 5.4 slice-start.3
  500.6 5.4 copy-start.42
  500.6 5.4 copy-start.47
  506.0 3.4 copy-start.14
  506.1 3.3 copy-start.8
  506.1 3.3 copy-start.51
  509.4 3.0 copy-start.21
  516.4 3.8 copy-start.1
  525.0 5.3 copy-start.31
  530.4 4.9 copy-start.18
  530.4 4.9 copy-start.24
  548.7 7.2 copy-start.10
  580.5 320.2 %reduce-scatter.8.cloned.1.call-start = ((), (), s32[]{:S(2)}) async-start(), calls=%async_computation.11 | async-start | bytes 7962624 | tf_op jit(solution)/shard_map/reduce_scatter | solution.py:195
  587.8 474.6 %reduce-scatter.4.cloned.1.call-start = ((), (), s32[]{:S(2)}) async-start(), calls=%async_computation.9 | async-start | bytes 17915904 | tf_op jit(solution)/shard_map/reduce_scatter | solution.py:297
  588.8 6.8 copy-start.4
  600.9 3.4 copy-start.40
  612.3 589.4 %all-reduce.12.cloned.1.call-start = ((), (), s32[]{:S(2)}) async-start(), calls=%async_computation.12 | async-start | bytes 11943936 | tf_op jit(solution)/shard_map/psum | solution.py:322
  1201.7 3.8 copy-start.32
  (31 other events, 43.7 us)
Sparse Core Ops, SparseCore 0:
  9.7 147.2 all-gather.6
  158.6 76.7 all-gather.8
  237.0 32.7 all-gather.10
  271.3 70.2 all-gather.12
  343.1 69.8 all-gather.14
  414.5 69.8 all-gather.16
  580.6 242.0 reduce-scatter.5
  825.1 75.5 reduce-scatter.7
  903.2 159.0 reduce-scatter.3
  1067.8 133.8 all-reduce.11
where the time goes:
time: 1230 us; the launch traced here: 1220 us
  waiting for transfers between devices  907 us (74%)
  matrix products  128 us (10%)
  blocking collectives  67.6 us (5%)
  other arithmetic  63.1 us (5%)
  local copies, waits for them, and re-layouts  33.2 us (3%)
  between operations  19.5 us (2%)
    reduce_scatter x1, waiting for transfers between devices, on_device(): lax.psum_scatter(jnp.concatenate([matmul_left_t(hidden_two, gate_back), m...  210 us
    reduce_scatter x1, waiting for transfers between devices, on_device(): lax.psum_scatter(matmul_left_t(back_flat, activated_flat).astype(jnp.bflo...  162 us
    all_gather x1, waiting for transfers between devices, on_device(): lax.all_gather(modulation_weight, 'fsdp', axis=1, tiled=True)  108 us
    psum x1, waiting for transfers between devices, on_device(): lax.psum(table_gradient.astype(jnp.bfloat16), 'rep').astype(jnp.float32)  89.7 us
    reduce_scatter x1, waiting for transfers between devices, on_device(): lax.psum_scatter(matmul_left_t(hidden_three, feed_back).astype(jnp.bfloat...  71.3 us
    all_gather x1, waiting for transfers between devices, on_device(): lax.all_gather(up_weight, 'fsdp', axis=0, tiled=True)  64.5 us
    all_gather x1, waiting for transfers between devices, on_device(): lax.all_gather(down_weight, 'fsdp', axis=0, tiled=True)  64.5 us
    all_gather x1, waiting for transfers between devices, on_device(): lax.all_gather(gate_weight, 'fsdp', axis=0, tiled=True)  64.2 us
  transfers between devices with their start and end apart: 10, of which 10 were waited for; matrix products, arithmetic and copies ran while one was open for 9% of the time, Pallas kernels for 0%

commit v1 on v0

v1 whole, which is shorter than its diff:
```python
import math

import jax
import jax.numpy as jnp
from jax import lax
from jax.sharding import PartitionSpec as P

HEADS = 16
BF = jnp.bfloat16
F32 = jnp.float32


def token_places(segment_ids, heights, widths):
    slot_count = heights.shape[1]
    token_count = segment_ids.shape[1]
    slot_ids = jnp.arange(slot_count, dtype=jnp.int32)
    member_ints = (segment_ids[:, :, None] == slot_ids[None, None, :]).astype(jnp.int32)
    before_ints = (slot_ids[None, None, :] < segment_ids[:, :, None]).astype(jnp.int32)
    grid_sizes = heights * widths
    starts = jnp.sum(before_ints * grid_sizes[:, None, :], axis=2)
    offsets = jnp.arange(token_count, dtype=jnp.int32)[None, :] - starts
    row_width = jnp.sum(member_ints * widths[:, None, :], axis=2)
    return (member_ints.astype(jnp.float32), offsets // row_width, offsets % row_width)


def rotary_tables(grid_rows, grid_columns, head_width):
    pair_count = head_width // 4
    frequency = 10000.0 ** (-jnp.arange(pair_count, dtype=jnp.float32) / pair_count)
    places = jnp.stack([grid_rows, grid_columns], axis=-1).astype(jnp.float32)
    turned = places[..., None] * frequency
    return (jnp.cos(turned)[:, :, None], jnp.sin(turned)[:, :, None])


def rotate(vectors, cosine_table, sine_table):
    full_shape = vectors.shape
    split_view = vectors.reshape(full_shape[:-1] + (2, 2, full_shape[-1] // 4))
    first_half = split_view[..., 0, :]
    second = split_view[..., 1, :]
    turned = jnp.stack(
        [
            first_half * cosine_table - second * sine_table,
            first_half * sine_table + second * cosine_table,
        ],
        axis=-2,
    )
    return turned.reshape(full_shape)


def normalize_keep(values):
    centered = values - jnp.mean(values, axis=-1, keepdims=True)
    variance = jnp.mean(centered * centered, axis=-1, keepdims=True)
    inverse = lax.rsqrt(variance + 1e-06)
    return (centered * inverse, inverse)


def normalize_back(normed, inverse, upstream):
    return inverse * (
        upstream
        - jnp.mean(upstream, axis=-1, keepdims=True)
        - normed * jnp.mean(upstream * normed, axis=-1, keepdims=True)
    )


def matmul(left, right):
    return jnp.dot(left, right, preferred_element_type=jnp.float32)


def matmul_right_t(left, right):
    return lax.dot_general(
        left, right, (((left.ndim - 1,), (1,)), ((), ())), preferred_element_type=jnp.float32
    )


def matmul_left_t(left, right):
    return lax.dot_general(
        left, right, (((0,), (0,)), ((), ())), preferred_element_type=jnp.float32
    )


def silu_slope(values):
    sigmoid = jax.nn.sigmoid(values)
    return sigmoid * (1.0 + values * (1.0 - sigmoid))


def swap_with(value, axis, size, bit):
    return lax.ppermute(value, axis, [(i, i ^ bit) for i in range(size)])


def bits_of(size):
    return [1 << k for k in range(size.bit_length() - 1)]


def reorder(blocks, index, size):
    rest = blocks.shape[1:]
    for bit in bits_of(size):
        paired = blocks.reshape((size // (2 * bit), 2, bit) + rest)
        flipped = jnp.stack([paired[:, 1], paired[:, 0]], axis=1)
        blocks = jnp.where((index & bit) != 0, flipped, paired).reshape((size,) + rest)
    return blocks


def hop_gather(value, axis, size):
    held = value
    for depth, bit in enumerate(reversed(bits_of(size))):
        held = jnp.stack([held, swap_with(held, axis, size, bit)], axis=depth)
    return held.reshape((size,) + value.shape)


def hop_exchange(blocks, axis, size):
    rest = blocks.shape[1:]
    for bit in bits_of(size):
        paired = blocks.reshape((size // (2 * bit), 2, bit) + rest)
        came = swap_with(paired[:, 1], axis, size, bit)
        blocks = jnp.stack([paired[:, 0], came], axis=1).reshape((size,) + rest)
    return blocks


def hop_scatter(blocks, axis, size):
    held = blocks
    for bit in bits_of(size):
        paired = held.reshape((held.shape[0] // 2, 2) + held.shape[1:])
        held = paired[:, 0] + swap_with(paired[:, 1], axis, size, bit)
    return held[0]


def hop_sum(value, axis, size):
    for bit in bits_of(size):
        value = value + swap_with(value, axis, size, bit)
    return value


def gather_blocks(value, axis, size):
    if size != 4:
        return jnp.stack(
            [value] + [swap_with(value, axis, size, j) for j in range(1, size)], axis=0
        )
    half = value.shape[-2] // 2
    top, low = value[..., :half, :], value[..., half:, :]
    top_one = swap_with(top, axis, size, 1)
    low_two = swap_with(low, axis, size, 2)
    low_one = swap_with(low, axis, size, 1)
    top_two = swap_with(top, axis, size, 2)
    top_three = swap_with(top_one, axis, size, 2)
    low_three = swap_with(low_two, axis, size, 1)
    return jnp.stack(
        [
            value,
            jnp.concatenate([top_one, low_one], axis=-2),
            jnp.concatenate([top_two, low_two], axis=-2),
            jnp.concatenate([top_three, low_three], axis=-2),
        ],
        axis=0,
    )


def exchange_blocks(blocks, axis, size):
    return jnp.stack(
        [blocks[0]] + [swap_with(blocks[j], axis, size, j) for j in range(1, size)], axis=0
    )


def scatter_blocks(blocks, axis, size):
    if size != 4:
        total = blocks[0]
        for j in range(1, size):
            total = total + swap_with(blocks[j].astype(BF), axis, size, j).astype(F32)
        return total
    half = blocks.shape[-2] // 2
    top, low = blocks[..., :half, :], blocks[..., half:, :]
    top_three = swap_with(top[3].astype(BF), axis, size, 1)
    low_three = swap_with(low[3].astype(BF), axis, size, 2)
    top_one = swap_with(top[1].astype(BF), axis, size, 1)
    low_two = swap_with(low[2].astype(BF), axis, size, 2)
    top_pair = (top[2] + top_three.astype(F32)).astype(BF)
    low_pair = (low[1] + low_three.astype(F32)).astype(BF)
    top_two = swap_with(top_pair, axis, size, 2)
    low_one = swap_with(low_pair, axis, size, 1)
    return jnp.concatenate(
        [
            top[0] + top_one.astype(F32) + top_two.astype(F32),
            low[0] + low_two.astype(F32) + low_one.astype(F32),
        ],
        axis=-2,
    )


def on_device(
    rep_size,
    fsdp_size,
    tokens,
    conditioning,
    segment_ids,
    heights,
    widths,
    pad_mask,
    modulation_weight,
    modulation_bias,
    projection_weight,
    projection_bias,
    output_weight,
    output_bias,
    gate_weight,
    up_weight,
    down_weight,
    cotangent,
):
    rows, token_count, width = tokens.shape
    slots = conditioning.shape[1]
    head_width = width // HEADS
    local_heads = HEADS // rep_size
    block = width // rep_size
    flat = rows * token_count
    all_rows = rep_size * rows
    all_flat = all_rows * token_count
    score_scale = 1.0 / math.sqrt(head_width)
    shard_ff = down_weight.shape[0]
    piece = shard_ff // rep_size
    block_ff = fsdp_size * piece
    shard_width = projection_weight.shape[0]
    columns = modulation_weight.shape[1]
    r = lax.axis_index("rep")
    f = lax.axis_index("fsdp")

    def rep_block(array, axis):
        return lax.dynamic_index_in_dim(array, r, axis, keepdims=False)

    qkv_shard = rep_block(
        projection_weight.reshape(shard_width, 3, rep_size, block), 2
    ).reshape(shard_width, 3 * block)
    qkv_block = lax.all_gather(qkv_shard, "fsdp", axis=0, tiled=True)
    out_full = lax.all_gather(output_weight, "fsdp", axis=0, tiled=True)
    gate_shard = rep_block(gate_weight.reshape(shard_width, fsdp_size, rep_size, piece), 2)
    up_shard = rep_block(up_weight.reshape(shard_width, fsdp_size, rep_size, piece), 2)
    gate_up_shard = jnp.concatenate(
        [gate_shard.reshape(shard_width, block_ff), up_shard.reshape(shard_width, block_ff)], axis=1
    )
    gate_up_block = lax.all_gather(gate_up_shard, "fsdp", axis=0, tiled=True)
    down_shard = rep_block(down_weight.reshape(rep_size, piece, width), 0)
    down_block = lax.all_gather(down_shard, "fsdp", axis=0, tiled=True)

    cond_float = conditioning.astype(F32)
    activated = jax.nn.silu(cond_float).astype(BF).reshape(rows * slots, width)
    bias_shard = jnp.concatenate([projection_bias, output_bias])
    bias_row = jnp.pad(bias_shard, (0, width - bias_shard.shape[0]))[None]
    gathered = hop_gather(jnp.concatenate([activated, bias_row], axis=0), "fsdp", fsdp_size)
    line_activated = gathered[:, : rows * slots]
    bias_all = reorder(gathered[:, rows * slots, : bias_shard.shape[0]], f, fsdp_size)
    projection_bias_all = bias_all[:, : projection_bias.shape[0]].reshape(3, rep_size, block)
    output_bias_all = bias_all[:, projection_bias.shape[0] :].reshape(width)
    line_modulation = matmul(
        line_activated.reshape(fsdp_size * rows * slots, width), modulation_weight
    ) + modulation_bias.astype(F32)
    own_modulation = reorder(
        hop_exchange(
            line_modulation.reshape(fsdp_size, rows * slots, columns), "fsdp", fsdp_size
        ),
        f,
        fsdp_size,
    )
    modulation = jnp.swapaxes(own_modulation, 0, 1).reshape(rows, slots, 6 * width)
    members, grid_rows, grid_columns = token_places(segment_ids, heights, widths)
    per_token = jnp.einsum("rsk,rkc->rsc", members, modulation, precision=lax.Precision.HIGHEST)
    shift_one, scale_one, gate_one, shift_two, scale_two, gate_two = jnp.split(
        per_token, 6, axis=-1
    )

    places = jnp.stack([segment_ids, grid_rows, grid_columns], axis=1)
    all_places = hop_gather(places, "rep", rep_size).reshape(all_rows, 3, token_count)
    all_segments = all_places[:, 0]
    cosine_table, sine_table = rotary_tables(all_places[:, 1], all_places[:, 2], head_width)
    tokens_float = tokens.astype(F32)
    normed_one, inverse_one = normalize_keep(tokens_float)
    hidden_one = (normed_one * (1.0 + scale_one) + shift_one).astype(BF)
    hidden_one_all = gather_blocks(hidden_one, "rep", rep_size).reshape(all_flat, width)
    masked = cotangent.astype(F32) * pad_mask.astype(F32)[:, :, None]
    feed_back = (gate_two * masked).astype(BF)
    feed_back_all = gather_blocks(feed_back, "rep", rep_size).reshape(all_flat, width)

    projected = matmul(hidden_one_all, qkv_block) + rep_block(projection_bias_all, 1).reshape(
        3 * block
    ).astype(F32)
    query_part, key_part, value_part = jnp.split(
        projected.reshape(all_rows, token_count, 3 * block), 3, axis=-1
    )
    head_shape = (all_rows, token_count, local_heads, head_width)
    query_rot = rotate(query_part.reshape(head_shape), cosine_table, sine_table).astype(BF)
    key_rot = rotate(key_part.reshape(head_shape), cosine_table, sine_table).astype(BF)
    value_low = value_part.reshape(head_shape).astype(BF)
    same_image = (all_segments[:, :, None] == all_segments[:, None, :])[:, None]
    raw_scores = (
        jnp.einsum("rqhe,rkhe->rhqk", query_rot, key_rot, preferred_element_type=F32) * score_scale
    )
    scores = jnp.where(same_image, raw_scores, -1e30)
    exponent = jnp.exp(scores - jnp.max(scores, axis=-1, keepdims=True))
    attention_probs = exponent / jnp.sum(exponent, axis=-1, keepdims=True)
    probs_low = attention_probs.astype(BF)
    attended_heads = jnp.einsum(
        "rhqk,rkhe->rqhe", probs_low, value_low, preferred_element_type=F32
    ).astype(BF)
    attended_blocks = reorder(
        exchange_blocks(
            attended_heads.reshape(rep_size, flat, block), "rep", rep_size
        ),
        r,
        rep_size,
    )
    attended = jnp.swapaxes(attended_blocks, 0, 1).reshape(flat, width)

    branch = (matmul(attended, out_full) + output_bias_all.astype(F32)).reshape(
        rows, token_count, width
    )
    middle = tokens_float + gate_one * branch
    normed_two, inverse_two = normalize_keep(middle)
    hidden_two = (normed_two * (1.0 + scale_two) + shift_two).astype(BF)
    hidden_two_all = gather_blocks(hidden_two, "rep", rep_size).reshape(all_flat, width)

    gate_block, up_block = gate_up_block[:, :block_ff], gate_up_block[:, block_ff:]
    gate_value = matmul(hidden_two_all, gate_block)
    up_value = matmul(hidden_two_all, up_block)
    hidden_three = (jax.nn.silu(gate_value) * up_value).astype(BF)
    hidden_back = matmul_right_t(feed_back_all, down_block)
    gate_back = (hidden_back * up_value * silu_slope(gate_value)).astype(BF)
    up_back = (hidden_back * jax.nn.silu(gate_value)).astype(BF)
    hidden_two_back_part = matmul_right_t(gate_back, gate_block) + matmul_right_t(up_back, up_block)
    hidden_two_back = scatter_blocks(
        hidden_two_back_part.reshape(rep_size, flat, width), "rep", rep_size
    ).reshape(rows, token_count, width)
    down_gradient = lax.psum_scatter(
        matmul_left_t(hidden_three, feed_back_all).astype(BF),
        "fsdp",
        scatter_dimension=0,
        tiled=True,
    )
    gate_up_gradient = lax.psum_scatter(
        jnp.concatenate(
            [matmul_left_t(hidden_two_all, gate_back), matmul_left_t(hidden_two_all, up_back)],
            axis=1,
        ).astype(BF),
        "fsdp",
        scatter_dimension=0,
        tiled=True,
    )
    feed = scatter_blocks(
        matmul(hidden_three, down_block).reshape(rep_size, flat, width), "rep", rep_size
    ).reshape(rows, token_count, width)
    block_output = (middle + gate_two * feed).astype(BF)
    gate_two_back = masked * feed

    middle_back = masked + normalize_back(
        normed_two, inverse_two, hidden_two_back * (1.0 + scale_two)
    )
    gate_one_back = middle_back * branch
    branch_back = (middle_back * gate_one).astype(BF).reshape(flat, width)
    attended_back_own = matmul_right_t(branch_back, out_full).astype(BF)
    attended_back = exchange_blocks(
        reorder(
            jnp.swapaxes(attended_back_own.reshape(flat, rep_size, block), 0, 1), r, rep_size
        ),
        "rep",
        rep_size,
    ).reshape(head_shape)
    output_gradient = hop_sum(
        lax.psum_scatter(
            matmul_left_t(attended, branch_back).astype(BF),
            "fsdp",
            scatter_dimension=0,
            tiled=True,
        ),
        "rep",
        rep_size,
    ).astype(F32)

    probs_back = jnp.einsum(
        "rqhe,rkhe->rhqk", attended_back, value_low, preferred_element_type=F32
    )
    value_back = jnp.einsum(
        "rhqk,rqhe->rkhe", probs_low, attended_back, preferred_element_type=F32
    )
    scores_back = (
        attention_probs
        * (probs_back - jnp.sum(attention_probs * probs_back, axis=-1, keepdims=True))
    ).astype(BF)
    query_back = (
        jnp.einsum("rhqk,rkhe->rqhe", scores_back, key_rot, preferred_element_type=F32)
        * score_scale
    )
    key_back = (
        jnp.einsum("rhqk,rqhe->rkhe", scores_back, query_rot, preferred_element_type=F32)
        * score_scale
    )
    query_back = rotate(query_back, cosine_table, -sine_table)
    key_back = rotate(key_back, cosine_table, -sine_table)
    projected_back = jnp.concatenate(
        [
            query_back.reshape(all_flat, block),
            key_back.reshape(all_flat, block),
            value_back.reshape(all_flat, block),
        ],
        axis=-1,
    ).astype(BF)
    hidden_one_back = scatter_blocks(
        matmul_right_t(projected_back, qkv_block).reshape(rep_size, flat, width), "rep", rep_size
    ).reshape(rows, token_count, width)
    projection_gradient = lax.psum_scatter(
        matmul_left_t(hidden_one_all, projected_back).astype(BF),
        "fsdp",
        scatter_dimension=0,
        tiled=True,
    )
    tokens_gradient = middle_back + normalize_back(
        normed_one, inverse_one, hidden_one_back * (1.0 + scale_one)
    )

    per_token_back = jnp.concatenate(
        [
            hidden_one_back,
            hidden_one_back * normed_one,
            gate_one_back,
            hidden_two_back,
            hidden_two_back * normed_two,
            gate_two_back,
        ],
        axis=-1,
    )
    modulation_back = jnp.einsum(
        "rsk,rsc->rkc", members, per_token_back, precision=lax.Precision.HIGHEST
    ).astype(BF)
    back_blocks = reorder(
        jnp.swapaxes(
            modulation_back.reshape(rows * slots, fsdp_size, columns), 0, 1
        ),
        f,
        fsdp_size,
    )
    line_back = hop_exchange(back_blocks, "fsdp", fsdp_size)
    all_back = hop_gather(line_back, "rep", rep_size).reshape(-1, columns)
    all_activated = hop_gather(line_activated, "rep", rep_size).reshape(-1, width)
    table_gradient = matmul_left_t(all_activated, all_back)
    table_bias_gradient = jnp.sum(all_back.astype(F32), axis=0)
    activated_back = hop_scatter(
        matmul_right_t(line_back.reshape(-1, columns), modulation_weight).reshape(
            fsdp_size, rows * slots, width
        ),
        "fsdp",
        fsdp_size,
    )
    conditioning_gradient = activated_back.reshape(rows, slots, width) * silu_slope(cond_float)

    def all_blocks(value):
        return reorder(gather_blocks(value, "rep", rep_size), r, rep_size).astype(F32)

    down_gradient = all_blocks(down_gradient).reshape(shard_ff, width)
    gate_up_gradient = all_blocks(gate_up_gradient).reshape(
        rep_size, shard_width, 2, fsdp_size, piece
    )
    gate_up_gradient = jnp.transpose(gate_up_gradient, (2, 1, 3, 0, 4)).reshape(
        2, shard_width, fsdp_size * shard_ff
    )
    projection_gradient = jnp.transpose(
        all_blocks(projection_gradient).reshape(rep_size, shard_width, 3, block), (1, 2, 0, 3)
    ).reshape(shard_width, 3 * width)
    bias_sums = hop_sum(
        jnp.concatenate(
            [
                jnp.sum(projected_back.astype(F32), axis=0),
                jnp.sum(branch_back.astype(F32), axis=0),
            ]
        ),
        "fsdp",
        fsdp_size,
    )
    bias_sums = reorder(hop_gather(bias_sums, "rep", rep_size), r, rep_size)
    projection_bias_gradient = jnp.swapaxes(
        bias_sums[:, : 3 * block].reshape(rep_size, 3, block), 0, 1
    ).reshape(fsdp_size, -1)
    output_bias_gradient = jnp.sum(bias_sums[:, 3 * block :], axis=0).reshape(fsdp_size, -1)
    return (
        block_output,
        tokens_gradient,
        conditioning_gradient,
        table_gradient,
        table_bias_gradient,
        projection_gradient,
        lax.dynamic_index_in_dim(projection_bias_gradient, f, 0, keepdims=False),
        output_gradient,
        lax.dynamic_index_in_dim(output_bias_gradient, f, 0, keepdims=False),
        gate_up_gradient[0],
        gate_up_gradient[1],
        down_gradient,
    )


def solution(mesh):
    sizes = dict(mesh.shape)

    def body(*arrays):
        return on_device(sizes["rep"], sizes["fsdp"], *arrays)

    rows = ("rep", "fsdp")
    in_specs = (
        P(rows, None, None),
        P(rows, None, None),
        P(rows, None),
        P(rows, None),
        P(rows, None),
        P(rows, None),
        P(None, "fsdp"),
        P("fsdp"),
        P("fsdp", None),
        P("fsdp"),
        P("fsdp", None),
        P("fsdp"),
        P("fsdp", None),
        P("fsdp", None),
        P("fsdp", None),
        P(rows, None, None),
    )
    out_specs = (
        P(rows, None, None),
        P(rows, None, None),
        P(rows, None, None),
        P(None, "fsdp"),
        P("fsdp"),
        P("fsdp", None),
        P("fsdp"),
        P("fsdp", None),
        P("fsdp"),
        P("fsdp", None),
        P("fsdp", None),
        P("fsdp", None),
    )
    return jax.shard_map(
        body, mesh=mesh, in_specs=in_specs, out_specs=out_specs, check_vma=False
    )
```

time: 1230 us -> 527 us (0.43)
  waiting for transfers between devices: 907 us -> 144 us
  starting transfers between devices: 0.6 us -> 96.4 us
  local copies, waits for them, and re-layouts: 33.2 us -> 125 us
  blocking collectives: 67.6 us -> 0 us
  matrix products: 128 us -> 81.9 us
    reduce_scatter x3, waiting for transfers between devices: 443 us -> 0.01 us  [the longest x1 0.01 us: on_device(): lax.psum_scatter(matmul_left_t(hidden_three, feed_back_all).astype(BF), '...]
    all_gather x6 -> x4, waiting for transfers between devices: 370 us -> 0.01 us  [the longest x1 0.01 us: on_device(): qkv_block = lax.all_gather(qkv_shard, 'fsdp', axis=0, tiled=True)]
    ppermute x0 -> x85, waiting for transfers between devices: none -> 143 us  [swap_with(): return lax.ppermute(value, axis, [(i, i ^ bit) for i in range(size)])]
    ppermute x0 -> x85, starting transfers between devices: none -> 95.6 us  [swap_with(): return lax.ppermute(value, axis, [(i, i ^ bit) for i in range(size)])]
    psum x1 -> x0, waiting for transfers between devices: 89.7 us -> none  [on_device(): lax.psum(table_gradient.astype(jnp.bfloat16), 'rep').astype(jnp.float32)]
    unnamed x2 -> x0, blocking collectives: 57.3 us -> none
    reshape x0 -> x20, local copies, waits for them, and re-layouts: none -> 37.5 us  [the longest x1 16.3 us: on_device(): projected.reshape(all_rows, token_count, 3 * block)]
    dot_general x4 -> x2, matrix products: 20.2 us -> 1.27 us  [the longest x1 0.75 us: on_device(): jnp.einsum('rqhe,rkhe->rhqk', query_rot, key_rot, preferred_element_type=...]
  transfers between devices with their start and end apart: 10 -> 93, of which waited for: 10 -> 40; matrix products, arithmetic and copies ran while one was open for 9% -> 37% of each run, Pallas kernels for 0% -> 0%
where the time goes in v1:
time: 527 us; the launch traced here: 522 us
  waiting for transfers between devices  144 us (27%)
  local copies, waits for them, and re-layouts  125 us (24%)
  starting transfers between devices  96.4 us (18%)
  matrix products  81.9 us (16%)
  other arithmetic  58.4 us (11%)
  between operations  16.5 us (3%)
    ppermute x85, waiting for transfers between devices, swap_with(): return lax.ppermute(value, axis, [(i, i ^ bit) for i in range(size)])  143 us
    ppermute x85, starting transfers between devices, swap_with(): return lax.ppermute(value, axis, [(i, i ^ bit) for i in range(size)])  95.6 us
    dot_general x6, matrix products, matmul(): return jnp.dot(left, right, preferred_element_type=jnp.float32)  24.1 us
    unnamed x157, local copies, waits for them, and re-layouts  23.8 us
    dot_general x6, matrix products, matmul_left_t(): lax.dot_general(left, right, (((0,), (0,)), ((), ())), preferred_element_...  21.3 us
    dot_general x6, matrix products, matmul_right_t(): lax.dot_general(left, right, (((left.ndim - 1,), (1,)), ((), ())), prefer...  19.5 us
    reshape x1, local copies, waits for them, and re-layouts, on_device(): projected.reshape(all_rows, token_count, 3 * block)  16.3 us
    another operation x14, local copies, waits for them, and re-layouts, reorder(): flipped = jnp.stack([paired[:, 1], paired[:, 0]], axis=1)  10.6 us
  transfers between devices with their start and end apart: 93, of which 40 were waited for; matrix products, arithmetic and copies ran while one was open for 37% of the time, Pallas kernels for 0%

profile of v1, /device:TPU:0, one launch (start us, length us, event | category | flops | bytes accessed | tf_op | source)
XLA Modules:
  0.0 522.2 jit_solution(13983835484528642259)
XLA Ops:
  18.1 3.7 reshape.1405
  21.8 5.7 %dynamic-slice_reduce_fusion.1 = (bf16[144,8,96]{2,1,0:T(8,128)(2,1)}, bf16[144,8,96]{2,1,0:T(8,128)(2,1)S(1)}) fusion(bf16[144,8,4,96]{3,2,1,0:T(4,128)(2,1)S(1)} %reshape.1407, s32[]{:T(128)S(6)} %select_n.479, bf16[144,8,4,96]{3,2,1,0:T(4,128)(2,1)} %reshape.1405), kind=kLoop, calls=%fused_computation.190 | loop fusion | bytes 884740 | tf_op jit(solution)/shard_map/jit(dynamic_index_in_dim)/dynamic_slice | solution.py:225
  30.4 4.1 collective-permute-start
  58.8 5.8 %collective-permute-done.5 = f32[1,4,4,864]{3,2,1,0:T(4,128)S(1)} collective-permute-done((f32[1,4,4,864]{3,2,1,0:T(4,128)S(1)}, f32[1,4,4,864]{3,2,1,0:T(4,128)S(1)}, u32[]{:S(2)}, u32[]{:S(2)}) %collective-permute-start.5) | collective-permute-done | bytes 55328 | tf_op jit(solution)/shard_map/ppermute | solution.py:86
  65.1 5.6 %convolution_bitcast_fusion = f32[1,256,6912]{2,1,0:T(8,128)S(1)} fusion(f32[256,4]{1,0:T(8,128)S(1)} %bitcast.654, f32[4,6912]{1,0:T(4,128)S(1)} %reshape.1394), kind=kOutput, calls=%fused_computation.1 | convolution fusion | flops 84934656 | bytes 7192576 | tf_op jit(solution)/shard_map/rsk,rkc->rsc/dot_general | solution.py:262
  79.8 10.0 %collective-permute-done.9 = bf16[1,128,1152]{2,1,0:T(8,128)(2,1)} collective-permute-done((bf16[1,128,1152]{2,1,0:T(8,128)(2,1)S(1)}, bf16[1,128,1152]{2,1,0:T(8,128)(2,1)}, u32[]{:S(2)}, u32[]{:S(2)}) %collective-permute-start.9) | collective-permute-done | bytes 294944 | tf_op jit(solution)/shard_map/ppermute | solution.py:86
  93.2 3.5 collective-permute-done.11
  98.5 6.6 %convolution_add_fusion.2 = f32[1024,864]{0,1:T(8,128)} fusion(bf16[1024,1152]{1,0:T(8,128)(2,1)} %bitcast.630, bf16[1152,864]{1,0:T(8,128)(2,1)} %all-gather.6.cloned.1.call-done, f32[864]{0:T(1024)S(1)} %reshape.1443), kind=kOutput, calls=%fused_computation.43 | convolution fusion | flops 2039316480 | bytes 7892352 | tf_op jit(solution)/shard_map/dot_general | solution.py:65
  105.1 16.3 %reshape.1399 = f32[4,256,864]{1,0,2:T(4,128)} reshape(f32[1024,864]{0,1:T(8,128)} %convolution_add_fusion.2) | data formatting | bytes 7077888 | tf_op jit(solution)/shard_map/reshape | solution.py:283
  142.9 4.6 fusion.134
  155.4 10.6 %collective-permute-done.20 = bf16[1,128,1152]{2,1,0:T(8,128)(2,1)S(1)} collective-permute-done((bf16[1,128,1152]{2,1,0:T(8,128)(2,1)S(1)}, bf16[1,128,1152]{2,1,0:T(8,128)(2,1)S(1)}, u32[]{:S(2)}, u32[]{:S(2)}) %collective-permute-start.20) | collective-permute-done | bytes 294944 | tf_op jit(solution)/shard_map/ppermute | solution.py:86
  170.3 9.6 %collective-permute-done.32 = bf16[1,128,1152]{2,1,0:T(8,128)(2,1)S(1)} collective-permute-done((bf16[1,128,1152]{2,1,0:T(8,128)(2,1)S(1)}, bf16[1,128,1152]{2,1,0:T(8,128)(2,1)S(1)}, u32[]{:S(2)}, u32[]{:S(2)}) %collective-permute-start.32) | collective-permute-done | bytes 294944 | tf_op jit(solution)/shard_map/ppermute | solution.py:86
  193.5 6.2 %fusion.21 = f32[1024,768]{1,0:T(8,128)} fusion(bf16[1024,1152]{1,0:T(8,128)(2,1)} %bitcast.632, bf16[1152,1536]{1,0:T(8,128)(2,1)} %all-gather.10.cloned.1.call-done), kind=kOutput, calls=%fused_computation.60 | convolution fusion | flops 1811939328 | bytes 7274496 | tf_op jit(solution)/shard_map/dot_general | solution.py:65
  199.7 3.8 fusion.17
  203.5 7.3 %multiply_convert_fusion.1 = (bf16[1024,768]{1,0:T(8,128)(2,1)S(1)}, bf16[1024,768]{1,0:T(8,128)(2,1)S(1)}, bf16[1024,768]{1,0:T(8,128)(2,1)S(1)}) fusion(f32[1024,768]{1,0:T(8,128)} %fusion.21, f32[1024,768]{1,0:T(8,128)} %fusion.17, bf16[1024,1152]{1,0:T(8,128)(2,1)} %bitcast.636, bf16[1,768,1152]{2,1,0:T(8,128)(2,1)} %all-gather.12.cloned.1.call-done), kind=kOutput, calls=%fused_computation.25 | convolution fusion | flops 1823735808 | bytes 15138816 | tf_op jit(solution)/shard_map/dot_general | solution.py:69
  225.0 7.4 %collective-permute-done.24 = bf16[128,1152]{1,0:T(8,128)(2,1)S(1)} collective-permute-done((bf16[128,1152]{1,0:T(8,128)(2,1)S(1)}, bf16[128,1152]{1,0:T(8,128)(2,1)S(1)}, u32[]{:S(2)}, u32[]{:S(2)}) %collective-permute-start.24) | collective-permute-done | bytes 294944 | tf_op jit(solution)/shard_map/ppermute | solution.py:86
  235.7 5.5 %collective-permute-done.37 = bf16[128,1152]{1,0:T(8,128)(2,1)S(1)} collective-permute-done((bf16[128,1152]{1,0:T(8,128)(2,1)S(1)}, bf16[128,1152]{1,0:T(8,128)(2,1)S(1)}, u32[]{:S(2)}, u32[]{:S(2)}) %collective-permute-start.37) | collective-permute-done | bytes 294944 | tf_op jit(solution)/shard_map/ppermute | solution.py:86
  244.3 6.3 %collective-permute-done.25 = bf16[128,1152]{1,0:T(8,128)(2,1)S(1)} collective-permute-done((bf16[128,1152]{1,0:T(8,128)(2,1)S(1)}, bf16[128,1152]{1,0:T(8,128)(2,1)S(1)}, u32[]{:S(2)}, u32[]{:S(2)}) %collective-permute-start.25) | collective-permute-done | bytes 294944 | tf_op jit(solution)/shard_map/ppermute | solution.py:86
  252.7 4.9 collective-permute-done.28
  273.4 3.4 convolution_convert_fusion.3
  277.5 3.6 multiply_reduce_fusion
  292.3 4.0 convolution_convert_fusion.2
  296.3 3.7 convolution_convert_fusion.1
  301.8 3.4 collective-permute-done.56
  310.7 4.1 convolution_convert_fusion.4
  314.9 3.6 collective-permute-start.67
  326.0 6.2 %copy.378 = bf16[1152,1536]{1,0:T(8,128)(2,1)} copy(bf16[1152,1536]{0,1:T(8,128)(2,1)} %pad_maximum_fusion) | data formatting | bytes 7077888
  332.9 5.1 fusion.164
  343.8 5.7 %collective-permute-done.45 = bf16[128,1152]{1,0:T(8,128)(2,1)S(1)} collective-permute-done((bf16[128,1152]{1,0:T(8,128)(2,1)S(1)}, bf16[128,1152]{1,0:T(8,128)(2,1)S(1)}, u32[]{:S(2)}, u32[]{:S(2)}) %collective-permute-start.45) | collective-permute-done | bytes 294944 | tf_op jit(solution)/shard_map/ppermute | solution.py:86
  350.9 3.3 collective-permute-done.44
  354.1 7.6 %collective-permute-done.46 = bf16[128,1152]{1,0:T(8,128)(2,1)S(1)} collective-permute-done((bf16[128,1152]{1,0:T(8,128)(2,1)S(1)}, bf16[128,1152]{1,0:T(8,128)(2,1)S(1)}, u32[]{:S(2)}, u32[]{:S(2)}) %collective-permute-start.46) | collective-permute-done | bytes 294944 | tf_op jit(solution)/shard_map/ppermute | solution.py:86
  362.9 5.8 %collective-permute-done.49 = bf16[128,1152]{1,0:T(8,128)(2,1)S(1)} collective-permute-done((bf16[128,1152]{1,0:T(8,128)(2,1)S(1)}, bf16[128,1152]{1,0:T(8,128)(2,1)S(1)}, u32[]{:S(2)}, u32[]{:S(2)}) %collective-permute-start.49) | collective-permute-done | bytes 294944 | tf_op jit(solution)/shard_map/ppermute | solution.py:86
  375.6 3.4 convolution_convert_fusion
  381.7 3.4 collective-permute-done.51
  386.5 3.4 collective-permute-done.52
  404.7 3.8 convolution_bitcast_fusion.1
  437.1 4.8 stack.604
  445.3 3.2 convert_bitcast_fusion.1
  448.6 3.3 copy.350
  451.9 3.6 reshape.1446
  461.8 4.6 collective-permute-done.72
  468.4 11.4 %collective-permute-done.76 = bf16[72,1536]{0,1:T(8,128)(2,1)S(1)} collective-permute-done((bf16[72,1536]{0,1:T(8,128)(2,1)S(1)}, bf16[72,1536]{0,1:T(8,128)(2,1)S(1)}, u32[]{:S(2)}, u32[]{:S(2)}) %collective-permute-start.76) | collective-permute-done | bytes 221216 | tf_op jit(solution)/shard_map/ppermute | solution.py:86
  483.7 3.9 collective-permute-done.78
  493.2 3.4 fusion.135
  496.6 4.7 copy.357
  501.4 4.5 squeeze.168
  505.9 4.7 copy.358
  510.6 4.5 squeeze.169
  (584 shorter events, 248.1 us)
Async XLA Ops:
  7.2 91.3 %all-gather.6.cloned.1.call-start = ((), (), s32[]{:S(2)}) async-start(), calls=%async_computation.4 | async-start | bytes 2322432 | tf_op jit(solution)/shard_map/all_gather | solution.py:230
  14.4 128.5 %all-gather.8.cloned.1.call-start = ((), (), s32[]{:S(2)}) async-start(), calls=%async_computation.5 | async-start | bytes 2985984 | tf_op jit(solution)/shard_map/all_gather | solution.py:231
  15.1 178.4 %all-gather.10.cloned.1.call-start = ((), (), s32[]{:S(2)}) async-start(), calls=%async_computation.6 | async-start | bytes 3981312 | tf_op jit(solution)/shard_map/all_gather | solution.py:237
  29.9 173.7 %all-gather.12.cloned.1.call-start = ((), (), s32[]{:S(2)}) async-start(), calls=%async_computation.10 | async-start | bytes 1990656 | tf_op jit(solution)/shard_map/all_gather | solution.py:239
  30.4 12.4 %collective-permute-start = (bf16[5,1152]{1,0:T(8,128)(2,1)S(1)}, bf16[5,1152]{1,0:T(8,128)(2,1)S(1)}, u32[]{:S(2)}, u32[]{:S(2)}) collective-permute-start(bf16[5,1152]{1,0:T(8,128)(2,1)S(1)} %get-tuple-element.170), channel_id=1, source_target_pairs={{0,4},{1,5},{2,6},{3,7},{4,0},{5,1},{6,2},{7,3},{8,12},{9,13},{10,... | collective-permute-start | bytes 34568 | tf_op jit(solution)/shard_map/ppermute | solution.py:86
  38.1 359.4 %reduce-scatter.11.cloned.1.call-start = ((), (), s32[]{:S(2)}) async-start(), calls=%async_computation.9 | async-start | bytes 1990656 | tf_op jit(solution)/shard_map/reduce_scatter | solution.py:328
  74.8 14.9 %collective-permute-start.6 = (bf16[1,128,1152]{2,1,0:T(8,128)(2,1)}, bf16[1,128,1152]{2,1,0:T(8,128)(2,1)S(1)}, u32[]{:S(2)}, u32[]{:S(2)}) collective-permute-start(bf16[1,128,1152]{2,1,0:T(8,128)(2,1)} %get-tuple-element.114), channel_id=1, source_target_pairs={{0,8},{8,0},{16,24},{24,16},{1,9},{9,1},{17,25},{25,17},{2,10},{10... | collective-permute-start | bytes 884744 | tf_op jit(solution)/shard_map/ppermute | solution.py:86
  76.4 14.7 %collective-permute-start.8 = (bf16[1,128,1152]{2,1,0:T(8,128)(2,1)}, bf16[1,128,1152]{2,1,0:T(8,128)(2,1)}, u32[]{:S(2)}, u32[]{:S(2)}) collective-permute-start(bf16[1,128,1152]{2,1,0:T(8,128)(2,1)} %get-tuple-element.114), channel_id=1, source_target_pairs={{0,16},{8,24},{16,0},{24,8},{1,17},{9,25},{17,1},{25,9},{2,18},{10... | collective-permute-start | bytes 884744 | tf_op jit(solution)/shard_map/ppermute | solution.py:86
  77.5 12.2 %collective-permute-start.9 = (bf16[1,128,1152]{2,1,0:T(8,128)(2,1)S(1)}, bf16[1,128,1152]{2,1,0:T(8,128)(2,1)}, u32[]{:S(2)}, u32[]{:S(2)}) collective-permute-start(bf16[1,128,1152]{2,1,0:T(8,128)(2,1)S(1)} %get-tuple-element.115), channel_id=1, source_target_pairs={{0,16},{8,24},{16,0},{24,8},{1,17},{9,25},{17,1},{25,9},{2,18},{10... | collective-permute-start | bytes 884744 | tf_op jit(solution)/shard_map/ppermute | solution.py:86
  79.0 13.1 %collective-permute-start.7 = (bf16[1,128,1152]{2,1,0:T(8,128)(2,1)S(1)}, bf16[1,128,1152]{2,1,0:T(8,128)(2,1)}, u32[]{:S(2)}, u32[]{:S(2)}) collective-permute-start(bf16[1,128,1152]{2,1,0:T(8,128)(2,1)S(1)} %get-tuple-element.115), channel_id=1, source_target_pairs={{0,8},{8,0},{16,24},{24,16},{1,9},{9,1},{17,25},{25,17},{2,10},{10... | collective-permute-start | bytes 884744 | tf_op jit(solution)/shard_map/ppermute | solution.py:86
  150.3 17.8 %collective-permute-start.17 = (bf16[1,128,1152]{2,1,0:T(8,128)(2,1)S(1)}, bf16[1,128,1152]{2,1,0:T(8,128)(2,1)S(1)}, u32[]{:S(2)}, u32[]{:S(2)}) collective-permute-start(bf16[1,128,1152]{2,1,0:T(8,128)(2,1)S(1)} %get-tuple-element.102), channel_id=1, source_target_pairs={{0,8},{8,0},{16,24},{24,16},{1,9},{9,1},{17,25},{25,17},{2,10},{10... | collective-permute-start | bytes 884744 | tf_op jit(solution)/shard_map/ppermute | solution.py:86
  151.3 15.8 %collective-permute-start.19 = (bf16[1,128,1152]{2,1,0:T(8,128)(2,1)S(1)}, bf16[1,128,1152]{2,1,0:T(8,128)(2,1)S(1)}, u32[]{:S(2)}, u32[]{:S(2)}) collective-permute-start(bf16[1,128,1152]{2,1,0:T(8,128)(2,1)S(1)} %get-tuple-element.102), channel_id=1, source_target_pairs={{0,16},{8,24},{16,0},{24,8},{1,17},{9,25},{17,1},{25,9},{2,18},{10... | collective-permute-start | bytes 884744 | tf_op jit(solution)/shard_map/ppermute | solution.py:86
  152.2 13.8 %collective-permute-start.20 = (bf16[1,128,1152]{2,1,0:T(8,128)(2,1)S(1)}, bf16[1,128,1152]{2,1,0:T(8,128)(2,1)S(1)}, u32[]{:S(2)}, u32[]{:S(2)}) collective-permute-start(bf16[1,128,1152]{2,1,0:T(8,128)(2,1)S(1)} %get-tuple-element.103), channel_id=1, source_target_pairs={{0,16},{8,24},{16,0},{24,8},{1,17},{9,25},{17,1},{25,9},{2,18},{10... | collective-permute-start | bytes 884744 | tf_op jit(solution)/shard_map/ppermute | solution.py:86
  153.3 16.4 %collective-permute-start.18 = (bf16[1,128,1152]{2,1,0:T(8,128)(2,1)S(1)}, bf16[1,128,1152]{2,1,0:T(8,128)(2,1)S(1)}, u32[]{:S(2)}, u32[]{:S(2)}) collective-permute-start(bf16[1,128,1152]{2,1,0:T(8,128)(2,1)S(1)} %get-tuple-element.103), channel_id=1, source_target_pairs={{0,8},{8,0},{16,24},{24,16},{1,9},{9,1},{17,25},{25,17},{2,10},{10... | collective-permute-start | bytes 884744 | tf_op jit(solution)/shard_map/ppermute | solution.py:86
  154.5 26.4 %collective-permute-start.29 = (bf16[1,128,1152]{2,1,0:T(8,128)(2,1)S(1)}, bf16[1,128,1152]{2,1,0:T(8,128)(2,1)S(1)}, u32[]{:S(2)}, u32[]{:S(2)}) collective-permute-start(bf16[1,128,1152]{2,1,0:T(8,128)(2,1)S(1)} %get-tuple-element.100), channel_id=1, source_target_pairs={{0,8},{8,0},{16,24},{24,16},{1,9},{9,1},{17,25},{25,17},{2,10},{10... | collective-permute-start | bytes 884744 | tf_op jit(solution)/shard_map/ppermute | solution.py:86
  166.0 16.0 %collective-permute-start.31 = (bf16[1,128,1152]{2,1,0:T(8,128)(2,1)S(1)}, bf16[1,128,1152]{2,1,0:T(8,128)(2,1)S(1)}, u32[]{:S(2)}, u32[]{:S(2)}) collective-permute-start(bf16[1,128,1152]{2,1,0:T(8,128)(2,1)S(1)} %get-tuple-element.100), channel_id=1, source_target_pairs={{0,16},{8,24},{16,0},{24,8},{1,17},{9,25},{17,1},{25,9},{2,18},{10... | collective-permute-start | bytes 884744 | tf_op jit(solution)/shard_map/ppermute | solution.py:86
  167.0 12.8 %collective-permute-start.32 = (bf16[1,128,1152]{2,1,0:T(8,128)(2,1)S(1)}, bf16[1,128,1152]{2,1,0:T(8,128)(2,1)S(1)}, u32[]{:S(2)}, u32[]{:S(2)}) collective-permute-start(bf16[1,128,1152]{2,1,0:T(8,128)(2,1)S(1)} %get-tuple-element.101), channel_id=1, source_target_pairs={{0,16},{8,24},{16,0},{24,8},{1,17},{9,25},{17,1},{25,9},{2,18},{10... | collective-permute-start | bytes 884744 | tf_op jit(solution)/shard_map/ppermute | solution.py:86
  168.1 15.7 %collective-permute-start.30 = (bf16[1,128,1152]{2,1,0:T(8,128)(2,1)S(1)}, bf16[1,128,1152]{2,1,0:T(8,128)(2,1)S(1)}, u32[]{:S(2)}, u32[]{:S(2)}) collective-permute-start(bf16[1,128,1152]{2,1,0:T(8,128)(2,1)S(1)} %get-tuple-element.101), channel_id=1, source_target_pairs={{0,8},{8,0},{16,24},{24,16},{1,9},{9,1},{17,25},{25,17},{2,10},{10... | collective-permute-start | bytes 884744 | tf_op jit(solution)/shard_map/ppermute | solution.py:86
  169.7 14.2 %collective-permute-start.22 = (bf16[1,128,1152]{2,1,0:T(8,128)(2,1)S(1)}, bf16[1,128,1152]{2,1,0:T(8,128)(2,1)S(1)}, u32[]{:S(2)}, u32[]{:S(2)}) collective-permute-start(bf16[1,128,1152]{2,1,0:T(8,128)(2,1)S(1)} %collective-permute-done.20), channel_id=1, source_target_pairs={{0,8},{8,0},{16,24},{24,16},{1,9},{9,1},{17,25},{25,17},{2,10},{10... | collective-permute-start | bytes 884744 | tf_op jit(solution)/shard_map/ppermute | solution.py:86
  218.2 15.5 %collective-permute-start.35 = (bf16[128,1152]{1,0:T(8,128)(2,1)S(1)}, bf16[128,1152]{1,0:T(8,128)(2,1)S(1)}, u32[]{:S(2)}, u32[]{:S(2)}) collective-permute-start(bf16[128,1152]{1,0:T(8,128)(2,1)S(1)} %get-tuple-element.51), channel_id=1, source_target_pairs={{0,8},{8,0},{16,24},{24,16},{1,9},{9,1},{17,25},{25,17},{2,10},{10... | collective-permute-start | bytes 884744 | tf_op jit(solution)/shard_map/ppermute | solution.py:86
  218.3 16.3 %collective-permute-start.39 = (bf16[128,1152]{1,0:T(8,128)(2,1)S(1)}, bf16[128,1152]{1,0:T(8,128)(2,1)S(1)}, u32[]{:S(2)}, u32[]{:S(2)}) collective-permute-start(bf16[128,1152]{1,0:T(8,128)(2,1)S(1)} %get-tuple-element.52), channel_id=1, source_target_pairs={{0,16},{8,24},{16,0},{24,8},{1,17},{9,25},{17,1},{25,9},{2,18},{10... | collective-permute-start | bytes 884744 | tf_op jit(solution)/shard_map/ppermute | solution.py:86
  219.4 33.3 %collective-permute-start.38 = (bf16[128,1152]{1,0:T(8,128)(2,1)S(1)}, bf16[128,1152]{1,0:T(8,128)(2,1)S(1)}, u32[]{:S(2)}, u32[]{:S(2)}) collective-permute-start(bf16[128,1152]{1,0:T(8,128)(2,1)S(1)} %get-tuple-element.53), channel_id=1, source_target_pairs={{0,16},{8,24},{16,0},{24,8},{1,17},{9,25},{17,1},{25,9},{2,18},{10... | collective-permute-start | bytes 884744 | tf_op jit(solution)/shard_map/ppermute | solution.py:86
  222.9 9.6 %collective-permute-start.24 = (bf16[128,1152]{1,0:T(8,128)(2,1)S(1)}, bf16[128,1152]{1,0:T(8,128)(2,1)S(1)}, u32[]{:S(2)}, u32[]{:S(2)}) collective-permute-start(bf16[128,1152]{1,0:T(8,128)(2,1)S(1)} %get-tuple-element.58), channel_id=1, source_target_pairs={{0,8},{8,0},{16,24},{24,16},{1,9},{9,1},{17,25},{25,17},{2,10},{10... | collective-permute-start | bytes 884744 | tf_op jit(solution)/shard_map/ppermute | solution.py:86
  224.8 17.1 %collective-permute-start.23 = (bf16[128,1152]{1,0:T(8,128)(2,1)S(1)}, bf16[128,1152]{1,0:T(8,128)(2,1)S(1)}, u32[]{:S(2)}, u32[]{:S(2)}) collective-permute-start(bf16[128,1152]{1,0:T(8,128)(2,1)S(1)} %get-tuple-element.55), channel_id=1, source_target_pairs={{0,8},{8,0},{16,24},{24,16},{1,9},{9,1},{17,25},{25,17},{2,10},{10... | collective-permute-start | bytes 884744 | tf_op jit(solution)/shard_map/ppermute | solution.py:86
  232.5 8.7 %collective-permute-start.37 = (bf16[128,1152]{1,0:T(8,128)(2,1)S(1)}, bf16[128,1152]{1,0:T(8,128)(2,1)S(1)}, u32[]{:S(2)}, u32[]{:S(2)}) collective-permute-start(bf16[128,1152]{1,0:T(8,128)(2,1)S(1)} %fusion.64), channel_id=1, source_target_pairs={{0,16},{8,24},{16,0},{24,8},{1,17},{9,25},{17,1},{25,9},{2,18},{10... | collective-permute-start | bytes 884744 | tf_op jit(solution)/shard_map/ppermute | solution.py:86
  233.6 10.7 %collective-permute-start.27 = (bf16[128,1152]{1,0:T(8,128)(2,1)S(1)}, bf16[128,1152]{1,0:T(8,128)(2,1)S(1)}, u32[]{:S(2)}, u32[]{:S(2)}) collective-permute-start(bf16[128,1152]{1,0:T(8,128)(2,1)S(1)} %get-tuple-element.56), channel_id=1, source_target_pairs={{0,16},{8,24},{16,0},{24,8},{1,17},{9,25},{17,1},{25,9},{2,18},{10... | collective-permute-start | bytes 884744 | tf_op jit(solution)/shard_map/ppermute | solution.py:86
  234.6 18.1 %collective-permute-start.26 = (bf16[128,1152]{1,0:T(8,128)(2,1)S(1)}, bf16[128,1152]{1,0:T(8,128)(2,1)S(1)}, u32[]{:S(2)}, u32[]{:S(2)}) collective-permute-start(bf16[128,1152]{1,0:T(8,128)(2,1)S(1)} %get-tuple-element.57), channel_id=1, source_target_pairs={{0,16},{8,24},{16,0},{24,8},{1,17},{9,25},{17,1},{25,9},{2,18},{10... | collective-permute-start | bytes 884744 | tf_op jit(solution)/shard_map/ppermute | solution.py:86
  241.2 9.5 %collective-permute-start.25 = (bf16[128,1152]{1,0:T(8,128)(2,1)S(1)}, bf16[128,1152]{1,0:T(8,128)(2,1)S(1)}, u32[]{:S(2)}, u32[]{:S(2)}) collective-permute-start(bf16[128,1152]{1,0:T(8,128)(2,1)S(1)} %fusion.72), channel_id=1, source_target_pairs={{0,16},{8,24},{16,0},{24,8},{1,17},{9,25},{17,1},{25,9},{2,18},{10... | collective-permute-start | bytes 884744 | tf_op jit(solution)/shard_map/ppermute | solution.py:86
  242.0 10.7 %collective-permute-start.40 = (bf16[128,1152]{1,0:T(8,128)(2,1)S(1)}, bf16[128,1152]{1,0:T(8,128)(2,1)S(1)}, u32[]{:S(2)}, u32[]{:S(2)}) collective-permute-start(bf16[128,1152]{1,0:T(8,128)(2,1)S(1)} %get-tuple-element.36), channel_id=1, source_target_pairs={{0,8},{8,0},{16,24},{24,16},{1,9},{9,1},{17,25},{25,17},{2,10},{10... | collective-permute-start | bytes 884744 | tf_op jit(solution)/shard_map/ppermute | solution.py:86
  276.8 140.9 %reduce-scatter.7.cloned.1.call-start = ((), (), s32[]{:S(2)}) async-start(), calls=%async_computation.7 | async-start | bytes 2322432 | tf_op jit(solution)/shard_map/reduce_scatter | solution.py:404
  296.3 148.0 %reduce-scatter.9.cloned.1.call-start = ((), (), s32[]{:S(2)}) async-start(), calls=%async_computation.8 | async-start | bytes 2985984 | tf_op jit(solution)/shard_map/reduce_scatter | solution.py:363
  300.0 156.9 %reduce-scatter.13.cloned.1.call-start = ((), (), s32[]{:S(2)}) async-start(), calls=%async_computation.11 | async-start | bytes 3981312
  307.4 97.2 %collective-permute-start.57 = (bf16[2,8,4,1152]{3,1,2,0:T(8,128)(2,1)}, bf16[2,8,4,1152]{3,1,2,0:T(8,128)(2,1)}, u32[]{:S(2)}, u32[]{:S(2)}) collective-permute-start(bf16[2,8,4,1152]{3,1,2,0:T(8,128)(2,1)} %get-tuple-element.125), channel_id=1, source_target_pairs={{0,8},{8,0},{16,24},{24,16},{1,9},{9,1},{17,25},{25,17},{2,10},{10... | collective-permute-start | bytes 442376 | tf_op jit(solution)/shard_map/ppermute | solution.py:86
  320.8 11.4 %collective-permute-start.68 = (f32[2016]{0:T(1024)S(1)}, f32[2016]{0:T(1024)S(1)}, u32[]{:S(2)}, u32[]{:S(2)}) collective-permute-start(f32[2016]{0:T(1024)S(1)} %add.279), channel_id=1, source_target_pairs={{0,4},{1,5},{2,6},{3,7},{4,0},{5,1},{6,2},{7,3},{8,12},{9,13},{10,... | collective-permute-start | bytes 24200 | tf_op jit(solution)/shard_map/ppermute | solution.py:86
  339.5 10.0 %collective-permute-start.45 = (bf16[128,1152]{1,0:T(8,128)(2,1)S(1)}, bf16[128,1152]{1,0:T(8,128)(2,1)S(1)}, u32[]{:S(2)}, u32[]{:S(2)}) collective-permute-start(bf16[128,1152]{1,0:T(8,128)(2,1)S(1)} %get-tuple-element.50), channel_id=1, source_target_pairs={{0,8},{8,0},{16,24},{24,16},{1,9},{9,1},{17,25},{25,17},{2,10},{10... | collective-permute-start | bytes 884744 | tf_op jit(solution)/shard_map/ppermute | solution.py:86
  340.5 13.7 %collective-permute-start.44 = (bf16[128,1152]{1,0:T(8,128)(2,1)S(1)}, bf16[128,1152]{1,0:T(8,128)(2,1)S(1)}, u32[]{:S(2)}, u32[]{:S(2)}) collective-permute-start(bf16[128,1152]{1,0:T(8,128)(2,1)S(1)} %get-tuple-element.47), channel_id=1, source_target_pairs={{0,8},{8,0},{16,24},{24,16},{1,9},{9,1},{17,25},{25,17},{2,10},{10... | collective-permute-start | bytes 884744 | tf_op jit(solution)/shard_map/ppermute | solution.py:86
  341.6 12.6 %collective-permute-start.48 = (bf16[128,1152]{1,0:T(8,128)(2,1)S(1)}, bf16[128,1152]{1,0:T(8,128)(2,1)S(1)}, u32[]{:S(2)}, u32[]{:S(2)}) collective-permute-start(bf16[128,1152]{1,0:T(8,128)(2,1)S(1)} %get-tuple-element.48), channel_id=1, source_target_pairs={{0,16},{8,24},{16,0},{24,8},{1,17},{9,25},{17,1},{25,9},{2,18},{10... | collective-permute-start | bytes 884744 | tf_op jit(solution)/shard_map/ppermute | solution.py:86
  342.8 20.1 %collective-permute-start.47 = (bf16[128,1152]{1,0:T(8,128)(2,1)S(1)}, bf16[128,1152]{1,0:T(8,128)(2,1)S(1)}, u32[]{:S(2)}, u32[]{:S(2)}) collective-permute-start(bf16[128,1152]{1,0:T(8,128)(2,1)S(1)} %get-tuple-element.49), channel_id=1, source_target_pairs={{0,16},{8,24},{16,0},{24,8},{1,17},{9,25},{17,1},{25,9},{2,18},{10... | collective-permute-start | bytes 884744 | tf_op jit(solution)/shard_map/ppermute | solution.py:86
  349.5 12.2 %collective-permute-start.46 = (bf16[128,1152]{1,0:T(8,128)(2,1)S(1)}, bf16[128,1152]{1,0:T(8,128)(2,1)S(1)}, u32[]{:S(2)}, u32[]{:S(2)}) collective-permute-start(bf16[128,1152]{1,0:T(8,128)(2,1)S(1)} %fusion.56), channel_id=1, source_target_pairs={{0,16},{8,24},{16,0},{24,8},{1,17},{9,25},{17,1},{25,9},{2,18},{10... | collective-permute-start | bytes 884744 | tf_op jit(solution)/shard_map/ppermute | solution.py:86
  398.5 12.1 %collective-permute-start.79 = (bf16[48,1152]{1,0:T(8,128)(2,1)S(1)}, bf16[48,1152]{1,0:T(8,128)(2,1)S(1)}, u32[]{:S(2)}, u32[]{:S(2)}) collective-permute-start(bf16[48,1152]{1,0:T(8,128)(2,1)S(1)} %get-tuple-element.122), channel_id=1, source_target_pairs={{0,8},{8,0},{16,24},{24,16},{1,9},{9,1},{17,25},{25,17},{2,10},{10... | collective-permute-start | bytes 331784 | tf_op jit(solution)/shard_map/ppermute | solution.py:86
  399.7 11.7 %collective-permute-start.81 = (bf16[48,1152]{1,0:T(8,128)(2,1)S(1)}, bf16[48,1152]{1,0:T(8,128)(2,1)S(1)}, u32[]{:S(2)}, u32[]{:S(2)}) collective-permute-start(bf16[48,1152]{1,0:T(8,128)(2,1)S(1)} %get-tuple-element.122), channel_id=1, source_target_pairs={{0,16},{8,24},{16,0},{24,8},{1,17},{9,25},{17,1},{25,9},{2,18},{10... | collective-permute-start | bytes 331784 | tf_op jit(solution)/shard_map/ppermute | solution.py:86
  420.4 8.9 %collective-permute-start.62 = (bf16[72,864]{1,0:T(8,128)(2,1)}, bf16[72,864]{1,0:T(8,128)(2,1)}, u32[]{:S(2)}, u32[]{:S(2)}) collective-permute-start(bf16[72,864]{1,0:T(8,128)(2,1)} %get-tuple-element.121), channel_id=1, source_target_pairs={{0,16},{8,24},{16,0},{24,8},{1,17},{9,25},{17,1},{25,9},{2,18},{10... | collective-permute-start | bytes 373256 | tf_op jit(solution)/shard_map/ppermute | solution.py:86
  444.3 11.2 %collective-permute-start.71 = (bf16[144,1152]{1,0:T(8,128)(2,1)}, bf16[144,1152]{1,0:T(8,128)(2,1)S(1)}, u32[]{:S(2)}, u32[]{:S(2)}) collective-permute-start(bf16[144,1152]{1,0:T(8,128)(2,1)} %reduce-scatter.9.cloned.1.call-done), channel_id=1, source_target_pairs={{0,8},{8,0},{16,24},{24,16},{1,9},{9,1},{17,25},{25,17},{2,10},{10... | collective-permute-start | bytes 995336 | tf_op jit(solution)/shard_map/ppermute | solution.py:86
  455.6 10.8 %collective-permute-start.72 = (bf16[144,1152]{1,0:T(8,128)(2,1)S(1)}, bf16[144,1152]{1,0:T(8,128)(2,1)S(1)}, u32[]{:S(2)}, u32[]{:S(2)}) collective-permute-start(bf16[144,1152]{1,0:T(8,128)(2,1)S(1)} %add.282), channel_id=1, source_target_pairs={{0,16},{8,24},{16,0},{24,8},{1,17},{9,25},{17,1},{25,9},{2,18},{10... | collective-permute-start | bytes 995336 | tf_op jit(solution)/shard_map/ppermute | solution.py:86
  458.4 22.4 %collective-permute-start.73 = (bf16[72,1536]{0,1:T(8,128)(2,1)S(1)}, bf16[72,1536]{0,1:T(8,128)(2,1)S(1)}, u32[]{:S(2)}, u32[]{:S(2)}) collective-permute-start(bf16[72,1536]{0,1:T(8,128)(2,1)S(1)} %get-tuple-element.88), channel_id=1, source_target_pairs={{0,8},{8,0},{16,24},{24,16},{1,9},{9,1},{17,25},{25,17},{2,10},{10... | collective-permute-start | bytes 663560 | tf_op jit(solution)/shard_map/ppermute | solution.py:86
  459.8 23.2 %collective-permute-start.75 = (bf16[72,1536]{0,1:T(8,128)(2,1)S(1)}, bf16[72,1536]{0,1:T(8,128)(2,1)S(1)}, u32[]{:S(2)}, u32[]{:S(2)}) collective-permute-start(bf16[72,1536]{0,1:T(8,128)(2,1)S(1)} %get-tuple-element.88), channel_id=1, source_target_pairs={{0,16},{8,24},{16,0},{24,8},{1,17},{9,25},{17,1},{25,9},{2,18},{10... | collective-permute-start | bytes 663560 | tf_op jit(solution)/shard_map/ppermute | solution.py:86
  460.4 19.4 %collective-permute-start.76 = (bf16[72,1536]{0,1:T(8,128)(2,1)S(1)}, bf16[72,1536]{0,1:T(8,128)(2,1)S(1)}, u32[]{:S(2)}, u32[]{:S(2)}) collective-permute-start(bf16[72,1536]{0,1:T(8,128)(2,1)S(1)} %get-tuple-element.89), channel_id=1, source_target_pairs={{0,16},{8,24},{16,0},{24,8},{1,17},{9,25},{17,1},{25,9},{2,18},{10... | collective-permute-start | bytes 663560 | tf_op jit(solution)/shard_map/ppermute | solution.py:86
  467.3 16.0 %collective-permute-start.74 = (bf16[72,1536]{0,1:T(8,128)(2,1)S(1)}, bf16[72,1536]{0,1:T(8,128)(2,1)S(1)}, u32[]{:S(2)}, u32[]{:S(2)}) collective-permute-start(bf16[72,1536]{0,1:T(8,128)(2,1)S(1)} %get-tuple-element.89), channel_id=1, source_target_pairs={{0,8},{8,0},{16,24},{24,16},{1,9},{9,1},{17,25},{25,17},{2,10},{10... | collective-permute-start | bytes 663560 | tf_op jit(solution)/shard_map/ppermute | solution.py:86
  (117 other events, 743.2 us)
Sparse Core Ops, SparseCore 0:
  14.5 32.3 all-gather.5
  48.5 35.8 all-gather.7
  86.6 39.8 all-gather.9
  128.6 25.2 all-gather.11
  277.0 36.8 reduce-scatter.10
  316.0 34.1 reduce-scatter.6
  352.4 36.7 reduce-scatter.8
  391.6 43.1 reduce-scatter.12
